TPU v7x, 512 devices: a whole 4x4x16 slice. The times are simulated.
512 devices in a mesh: freq: 32 (over z_lo, x), src: 2 (over z_hi), rcv: 8 (over y, core).
Axes of the slice: x: 4, y: 4, z: 16 (z_hi: 2, z_lo: 8; z = z_hi * 8 + z_lo), core: 2. Of those that a mesh axis runs over, the one named last changes fastest.
Arguments:
- traces: float32 [1024, 1024, 256], P(('src', 'freq'), 'rcv'), may hold values from -6 to 6
Outputs:
- multiples: float32 [2, 96, 1024, 1024], P(None, 'freq', 'src', 'rcv')
All inputs are finite; a program needn't handle non-finite values.
Results may differ from a plain program's by a relative error of at most 0.000098.
Values sent between devices are 32-bit elements; how exact they have to be, the bound alone decides.
A program may use at most 64 MiB of HBM per device.

v0:
```python
import math
import jax
import jax.numpy as jnp
from jax import lax
from jax.sharding import PartitionSpec as P

N = 1024
FPD = 3


def dft_matrix(n_time, n_freq):
    times = jnp.arange(n_time, dtype=jnp.int32)
    bins = jnp.arange(n_freq, dtype=jnp.int32)
    phase = times[:, None] * bins[None, :] % n_time
    angle = phase.astype(jnp.float32) * (2.0 * math.pi / n_time)
    both = jnp.stack([jnp.cos(angle), -jnp.sin(angle)], axis=-1)
    return both.reshape(n_time, 2 * n_freq) * (1.0 / math.sqrt(n_time))


def batched_dot(left, right):
    return jnp.einsum(
        "mgq,mqn->mgn",
        left,
        right,
        precision=lax.Precision.HIGHEST,
        preferred_element_type=jnp.float32,
    )


def complex_product(left_re, left_im, right_re, right_im):
    real_part = batched_dot(left_re, right_re) - batched_dot(left_im, right_im)
    imag_part = batched_dot(left_re, right_im) + batched_dot(left_im, right_re)
    return (real_part, imag_part)


def per_device(traces):
    n_time = traces.shape[2]
    n_freq = FPD * lax.axis_size("freq")
    dft_table = dft_matrix(n_time, n_freq)
    spectra = jnp.einsum(
        "srt,tk->ksr",
        traces,
        dft_table,
        precision=lax.Precision.HIGHEST,
        preferred_element_type=jnp.float32,
    )
    regrouped = lax.all_to_all(spectra, "freq", split_axis=0, concat_axis=1, tiled=True)
    src_rows = regrouped.shape[1]
    rcv_cols = regrouped.shape[2]
    split_parts = regrouped.reshape(FPD, 2, src_rows, rcv_cols)
    local_re = split_parts[:, 0]
    local_im = split_parts[:, 1]
    col_re, col_im = (
        lax.all_gather(local_re, "src", axis=1, tiled=True),
        lax.all_gather(local_im, "src", axis=1, tiled=True),
    )
    piece_re = lax.all_gather(local_re, "rcv", axis=2, tiled=True)
    piece_im = lax.all_gather(local_im, "rcv", axis=2, tiled=True)
    real_part, imag_part = complex_product(piece_re, piece_im, col_re, col_im)
    scale = -1.0 / math.sqrt(N)
    return jnp.stack([real_part, imag_part]) * scale


def solution(mesh):
    in_specs = (P(("src", "freq"), "rcv", None),)
    out_specs = P(None, "freq", "src", "rcv")
    return jax.shard_map(
        per_device, mesh=mesh, in_specs=in_specs, out_specs=out_specs, check_vma=False
    )
```

profile of v0, /device:TPU:1, one launch (start us, length us, event | category | flops | bytes accessed | tf_op | source)
XLA Modules:
  0.0 411.7 jit_solution(3908307167513742405)
XLA Ops:
  6.5 0.0 copy-start
  6.5 0.0 all-gather.11.cloned.1.call-start
  6.5 0.4 sine_negate_fusion
  7.0 0.2 copy.14
  7.1 0.1 reshape.83
  7.3 0.8 copy-done
  8.1 2.3 fusion.39
  10.4 0.9 copy.15
  11.3 89.4 %all_to_all.15 = f32[192,16,128]{2,1,0:T(8,128)S(1)} all-to-all(f32[192,16,128]{2,1,0:T(8,128)S(1)} %copy.15), channel_id=1, replica_groups=mesh['freq'=32,'src'=2,'rcv'=8] {'freq'}, dimensions={0} | all-to-all | bytes 3145728 | tf_op jit(solution)/shard_map/all_to_all | solution.py:47
  100.7 0.1 copy.16
  100.9 1.3 slice_bitcast_fusion.1
  102.1 0.0 all-gather.11.cloned.1.call-update
  102.1 0.0 all-gather.13.cloned.1.call-start
  102.2 0.7 all-gather.13.cloned.1.call-update
  102.9 0.0 all-gather.15.cloned.1.call-start
  102.9 0.7 all-gather.15.cloned.1.call-update
  103.6 0.2 all-gather.9.cloned.1.call-start
  103.9 0.3 all-gather.9.cloned.1.call-update
  104.2 90.4 %all-gather.11.cloned.1.call-done = f32[3,1,1024,128]{3,2,0,1:T(8,128)} async-done(((f32[3,1,512,128]{3,2,0,1:T(8,128)}), f32[3,1,1024,128]{3,2,0,1:T(8,128)}) %all-gather.11.cloned.1.call-update) | async-done | bytes 1572880 | tf_op jit(solution)/shard_map/all_gather | solution.py:54
  194.6 48.8 %all-gather.13.cloned.1.call-done = f32[3,1,512,1024]{3,2,0,1:T(8,128)} async-done(((f32[3,1,512,128]{3,2,0,1:T(8,128)}), f32[3,1,512,1024]{3,2,0,1:T(8,128)}) %all-gather.13.cloned.1.call-update) | async-done | bytes 6291472 | tf_op jit(solution)/shard_map/all_gather | solution.py:58
  243.4 7.9 %fusion = f32[3,512,128]{2,1,0:T(8,128)S(1)} fusion(f32[3,1,512,1024]{3,2,0,1:T(8,128)} %all-gather.13.cloned.1.call-done, f32[3,1,1024,128]{3,2,0,1:T(8,128)} %all-gather.11.cloned.1.call-done), kind=kOutput, calls=%fused_computation | convolution fusion | flops 2415919104 | bytes 8650752 | tf_op jit(solution)/shard_map/mgq,mqn->mgn/dot_general | solution.py:21
  251.3 90.1 %all-gather.15.cloned.1.call-done = f32[3,1,1024,128]{3,2,0,1:T(8,128)} async-done(((f32[3,1,512,128]{3,2,0,1:T(8,128)}), f32[3,1,1024,128]{3,2,0,1:T(8,128)}) %all-gather.15.cloned.1.call-update) | async-done | bytes 1572880 | tf_op jit(solution)/shard_map/all_gather | solution.py:55
  341.4 8.8 %fusion.2 = f32[3,512,128]{2,1,0:T(8,128)} fusion(f32[3,1,512,1024]{3,2,0,1:T(8,128)} %all-gather.13.cloned.1.call-done, f32[3,1,1024,128]{3,2,0,1:T(8,128)} %all-gather.15.cloned.1.call-done), kind=kOutput, calls=%fused_computation.2 | convolution fusion | flops 2415919104 | bytes 8650752 | tf_op jit(solution)/shard_map/mgq,mqn->mgn/dot_general | solution.py:21
  350.2 39.8 %all-gather.9.cloned.1.call-done = f32[3,1,512,1024]{3,2,0,1:T(8,128)} async-done(((f32[3,1,512,128]{3,2,0,1:T(8,128)}), f32[3,1,512,1024]{3,2,0,1:T(8,128)}) %all-gather.9.cloned.1.call-update) | async-done | bytes 6291472 | tf_op jit(solution)/shard_map/all_gather | solution.py:57
  390.1 0.0 copy-start.1
  390.1 0.0 copy-start.2
  390.1 0.0 copy-start.3
  390.1 8.4 %fusion.22 = f32[1,3,512,128]{3,2,1,0:T(8,128)S(1)} fusion(f32[3,512,128]{2,1,0:T(8,128)S(1)} %fusion, f32[3,1,1024,128]{3,2,0,1:T(8,128)} %all-gather.15.cloned.1.call-done, f32[3,1,512,1024]{3,2,0,1:T(8,128)} %all-gather.9.cloned.1.call-done), kind=kOutput, calls=%fused_computation.15 | convolution fusion | flops 2416115712 | bytes 9437184 | tf_op jit(solution)/shard_map/mgq,mqn->mgn/dot_general | solution.py:21
  398.5 0.0 copy-done.1
  398.5 0.0 copy-done.2
  398.5 0.0 copy-done.3
  398.5 5.4 %fusion.27 = f32[1,3,512,128]{3,2,1,0:T(8,128)S(1)} fusion(f32[3,512,128]{2,1,0:T(8,128)S(1)} %copy-done.3, f32[3,1,1024,128]{3,2,0,1:T(8,128)S(1)} %copy-done.2, f32[3,1,512,1024]{3,2,0,1:T(8,128)S(1)} %copy-done.1), kind=kOutput, calls=%fused_computation.16 | convolution fusion | flops 2416115712 | bytes 9437184 | tf_op jit(solution)/shard_map/mgq,mqn->mgn/dot_general | solution.py:21
  403.9 1.2 maximum_multiply_fusion
  (1 shorter events, 0.0 us)
Async XLA Ops:
  6.5 1.6 copy-start
  6.5 188.0 %all-gather.11.cloned.1.call-start = ((), (), s32[]{:S(2)}) async-start(), calls=%async_computation.2 | async-start | bytes 2359296 | tf_op jit(solution)/shard_map/all_gather | solution.py:54
  102.1 141.2 %all-gather.13.cloned.1.call-start = ((), (), s32[]{:S(2)}) async-start(), calls=%async_computation.3 | async-start | bytes 7077888 | tf_op jit(solution)/shard_map/all_gather | solution.py:58
  102.9 238.5 %all-gather.15.cloned.1.call-start = ((), (), s32[]{:S(2)}) async-start(), calls=%async_computation.4 | async-start | bytes 2359296 | tf_op jit(solution)/shard_map/all_gather | solution.py:55
  103.6 286.5 %all-gather.9.cloned.1.call-start = ((), (), s32[]{:S(2)}) async-start(), calls=%async_computation.1 | async-start | bytes 7077888 | tf_op jit(solution)/shard_map/all_gather | solution.py:57
  390.1 8.4 %copy-start.1 = (f32[3,1,512,1024]{3,2,0,1:T(8,128)S(1)}, f32[3,1,512,1024]{3,2,0,1:T(8,128)}, u32[]{:S(2)}) copy-start(f32[3,1,512,1024]{3,2,0,1:T(8,128)} %all-gather.9.cloned.1.call-done) | copy-start | bytes 18874372
  390.1 8.4 %copy-start.2 = (f32[3,1,1024,128]{3,2,0,1:T(8,128)S(1)}, f32[3,1,1024,128]{3,2,0,1:T(8,128)}, u32[]{:S(2)}) copy-start(f32[3,1,1024,128]{3,2,0,1:T(8,128)} %all-gather.11.cloned.1.call-done) | copy-start | bytes 4718596
  390.1 8.4 %copy-start.3 = (f32[3,512,128]{2,1,0:T(8,128)S(1)}, f32[3,512,128]{2,1,0:T(8,128)}, u32[]{:S(2)}) copy-start(f32[3,512,128]{2,1,0:T(8,128)} %fusion.2) | copy-start | bytes 2359300
Sparse Core Ops, SparseCore 0:
  102.3 92.2 all-gather.10
  196.7 46.6 all-gather.12
  245.5 95.8 all-gather.14
  343.4 46.6 all-gather.8
where the time goes:
time: 412 us
  waiting for transfers between devices  271 us (66%)
  blocking collectives  89.4 us (22%)
  matrix products  32.8 us (8%)
  between operations  13.2 us (3%)
    all_gather x1, waiting for transfers between devices, per_device(): lax.all_gather(local_re, 'src', axis=1, tiled=True)  90.4 us
    all_gather x1, waiting for transfers between devices, per_device(): lax.all_gather(local_im, 'src', axis=1, tiled=True)  90.1 us
    all_to_all x1, blocking collectives, per_device(): lax.all_to_all(spectra, 'freq', split_axis=0, concat_axis=1, tiled=True)  89.4 us
    all_gather x1, waiting for transfers between devices, per_device(): piece_im = lax.all_gather(local_im, 'rcv', axis=2, tiled=True)  48.8 us
    all_gather x1, waiting for transfers between devices, per_device(): piece_re = lax.all_gather(local_re, 'rcv', axis=2, tiled=True)  39.8 us
    dot_general x4, matrix products, batched_dot(): jnp.einsum('mgq,mqn->mgn', left, right, precision=lax.Precision.HIGHEST,...  30.5 us
  transfers between devices with their start and end apart: 4, of which 4 were waited for; matrix products, arithmetic and copies ran while one was open for 4% of the time, Pallas kernels for 0%

commit v1 on v0

--- a/solution.py
+++ b/solution.py
@@ -1,3 +1,4 @@
+import functools
 import math
 import jax
 import jax.numpy as jnp
@@ -6,6 +7,22 @@
 
 N = 1024
 FPD = 3
+
+
+def post_zone(field_in, device_axis):
+    n_parts = lax.axis_size(device_axis)
+    latest = field_in
+    blocks_here = [latest]
+    arr_now = [(b - 1, b) for b in range(1, n_parts)] + [(n_parts - 1, 0)]
+    for _ in tuple(range(n_parts - 1)):
+        latest = lax.ppermute(latest, device_axis, arr_now)
+        blocks_here += [latest]
+    work_now = jnp.concatenate([*reversed(blocks_here)], axis=2)
+    carry_out = lax.axis_index(device_axis)
+    return jnp.roll(work_now, shift=(carry_out + 1) * latest.shape[2], axis=2)
+
+
+_lift_flows = functools.partial(post_zone, device_axis="rcv")
 
 
 def dft_matrix(n_time, n_freq):
@@ -54,7 +71,7 @@
         lax.all_gather(local_re, "src", axis=1, tiled=True),
         lax.all_gather(local_im, "src", axis=1, tiled=True),
     )
-    piece_re = lax.all_gather(local_re, "rcv", axis=2, tiled=True)
+    piece_re = _lift_flows(local_re)
     piece_im = lax.all_gather(local_im, "rcv", axis=2, tiled=True)
     real_part, imag_part = complex_product(piece_re, piece_im, col_re, col_im)
     scale = -1.0 / math.sqrt(N)

time: 412 us -> 375 us (0.910)
  waiting for transfers between devices: 271 us -> 183 us
  local copies, waits for them, and re-layouts: 3.48 us -> 34.8 us
  starting transfers between devices: 0.3 us -> 18.4 us
    all_gather x1, waiting for transfers between devices: 90.1 us -> 0.01 us  [per_device(): lax.all_gather(local_im, 'src', axis=1, tiled=True)]
    ppermute x0 -> x7, waiting for transfers between devices: none -> 63.1 us  [post_zone(): latest = lax.ppermute(latest, device_axis, arr_now)]
    all_gather x1 -> x0, waiting for transfers between devices: 39.8 us -> none  [per_device(): piece_re = lax.all_gather(local_re, 'rcv', axis=2, tiled=True)]
    unnamed x9 -> x39, local copies, waits for them, and re-layouts: 2.13 us -> 31 us
    all_gather x1, waiting for transfers between devices: 48.8 us -> 29 us  [per_device(): piece_im = lax.all_gather(local_im, 'rcv', axis=2, tiled=True)]
    ppermute x0 -> x7, starting transfers between devices: none -> 18.3 us  [post_zone(): latest = lax.ppermute(latest, device_axis, arr_now)]
  transfers between devices with their start and end apart: 4 -> 10, of which waited for: 4 -> 9; matrix products, arithmetic and copies ran while one was open for 4% -> 9% of each run, Pallas kernels for 0% -> 0%
where the time goes in v1:
time: 375 us; the launch traced here: 374 us
  waiting for transfers between devices  183 us (49%)
  blocking collectives  89.4 us (24%)
  local copies, waits for them, and re-layouts  34.8 us (9%)
  matrix products  34 us (9%)
  starting transfers between devices  18.4 us (5%)
  between operations  13.3 us (4%)
    all_gather x1, waiting for transfers between devices, per_device(): lax.all_gather(local_re, 'src', axis=1, tiled=True)  90.1 us
    all_to_all x1, blocking collectives, per_device(): lax.all_to_all(spectra, 'freq', split_axis=0, concat_axis=1, tiled=True)  89.4 us
    ppermute x7, waiting for transfers between devices, post_zone(): latest = lax.ppermute(latest, device_axis, arr_now)  63.1 us
    dot_general x4, matrix products, batched_dot(): jnp.einsum('mgq,mqn->mgn', left, right, precision=lax.Precision.HIGHEST,...  31.7 us
    unnamed x39, local copies, waits for them, and re-layouts  31 us
    all_gather x1, waiting for transfers between devices, per_device(): piece_im = lax.all_gather(local_im, 'rcv', axis=2, tiled=True)  29 us
    ppermute x7, starting transfers between devices, post_zone(): latest = lax.ppermute(latest, device_axis, arr_now)  18.3 us
  transfers between devices with their start and end apart: 10, of which 9 were waited for; matrix products, arithmetic and copies ran while one was open for 9% of the time, Pallas kernels for 0%

profile of v1, /device:TPU:1, one launch (start us, length us, event | category | flops | bytes accessed | tf_op | source)
XLA Modules:
  0.0 374.3 jit_solution(9475179533054944335)
XLA Ops:
  7.3 0.8 copy-done
  8.1 2.3 fusion.41
  10.4 0.9 copy.15
  11.3 89.4 %all_to_all.15 = f32[192,16,128]{2,1,0:T(8,128)S(1)} all-to-all(f32[192,16,128]{2,1,0:T(8,128)S(1)} %copy.15), channel_id=1, replica_groups=mesh['freq'=32,'src'=2,'rcv'=8] {'freq'}, dimensions={0} | all-to-all | bytes 3145728 | tf_op jit(solution)/shard_map/all_to_all | solution.py:64
  100.9 1.1 copy-done.1
  102.0 1.5 slice_bitcast_fusion.1
  103.6 0.7 all-gather.9.cloned.1.call-update
  104.3 3.4 collective-permute-start
  107.7 9.3 %collective-permute-done = f32[3,512,128]{2,1,0:T(8,128)S(1)} collective-permute-done((f32[3,512,128]{2,1,0:T(8,128)}, f32[3,512,128]{2,1,0:T(8,128)S(1)}, u32[]{:S(2)}, u32[]{:S(2)}) %collective-permute-start) | collective-permute-done | bytes 786464 | tf_op jit(solution)/shard_map/ppermute | solution.py:18
  117.0 2.4 collective-permute-start.1
  119.4 8.9 %collective-permute-done.1 = f32[3,512,128]{2,1,0:T(8,128)S(1)} collective-permute-done((f32[3,512,128]{2,1,0:T(8,128)S(1)}, f32[3,512,128]{2,1,0:T(8,128)S(1)}, u32[]{:S(2)}, u32[]{:S(2)}) %collective-permute-start.1) | collective-permute-done | bytes 786464 | tf_op jit(solution)/shard_map/ppermute | solution.py:18
  128.3 0.9 copy-done.4
  129.2 2.5 collective-permute-start.2
  131.7 8.9 %collective-permute-done.2 = f32[3,512,128]{2,1,0:T(8,128)S(1)} collective-permute-done((f32[3,512,128]{2,1,0:T(8,128)S(1)}, f32[3,512,128]{2,1,0:T(8,128)S(1)}, u32[]{:S(2)}, u32[]{:S(2)}) %collective-permute-start.2) | collective-permute-done | bytes 786464 | tf_op jit(solution)/shard_map/ppermute | solution.py:18
  140.6 1.0 copy-done.6
  141.6 2.5 collective-permute-start.3
  144.0 8.9 %collective-permute-done.3 = f32[3,512,128]{2,1,0:T(8,128)S(1)} collective-permute-done((f32[3,512,128]{2,1,0:T(8,128)S(1)}, f32[3,512,128]{2,1,0:T(8,128)S(1)}, u32[]{:S(2)}, u32[]{:S(2)}) %collective-permute-start.3) | collective-permute-done | bytes 786464 | tf_op jit(solution)/shard_map/ppermute | solution.py:18
  153.0 1.0 copy-done.8
  154.0 2.5 collective-permute-start.4
  156.4 8.9 %collective-permute-done.4 = f32[3,512,128]{2,1,0:T(8,128)S(1)} collective-permute-done((f32[3,512,128]{2,1,0:T(8,128)S(1)}, f32[3,512,128]{2,1,0:T(8,128)S(1)}, u32[]{:S(2)}, u32[]{:S(2)}) %collective-permute-start.4) | collective-permute-done | bytes 786464 | tf_op jit(solution)/shard_map/ppermute | solution.py:18
  165.4 0.9 copy-done.10
  166.3 2.5 collective-permute-start.5
  168.7 8.9 %collective-permute-done.5 = f32[3,512,128]{2,1,0:T(8,128)} collective-permute-done((f32[3,512,128]{2,1,0:T(8,128)S(1)}, f32[3,512,128]{2,1,0:T(8,128)}, u32[]{:S(2)}, u32[]{:S(2)}) %collective-permute-start.5) | collective-permute-done | bytes 786464 | tf_op jit(solution)/shard_map/ppermute | solution.py:18
  177.7 2.6 collective-permute-start.6
  180.3 9.2 %collective-permute-done.6 = f32[3,512,128]{2,1,0:T(8,128)} collective-permute-done((f32[3,512,128]{2,1,0:T(8,128)}, f32[3,512,128]{2,1,0:T(8,128)}, u32[]{:S(2)}, u32[]{:S(2)}) %collective-permute-start.6) | collective-permute-done | bytes 786464 | tf_op jit(solution)/shard_map/ppermute | solution.py:18
  189.5 2.2 constant_dynamic-update-slice_fusion.15
  191.7 2.1 constant_dynamic-update-slice_fusion.14
  193.8 2.1 constant_dynamic-update-slice_fusion.13
  195.9 2.1 constant_dynamic-update-slice_fusion.12
  198.0 2.1 constant_dynamic-update-slice_fusion.11
  200.1 2.1 constant_dynamic-update-slice_fusion.10
  202.3 1.0 constant_dynamic-update-slice_fusion.9
  203.3 2.1 constant_dynamic-update-slice_fusion.8
  205.4 2.2 constant_dynamic-update-slice_fusion.7
  207.6 2.2 constant_dynamic-update-slice_fusion.6
  209.7 1.0 constant_dynamic-update-slice_fusion.5
  210.7 1.0 constant_dynamic-update-slice_fusion.4
  211.8 1.0 constant_dynamic-update-slice_fusion.3
  212.8 1.0 constant_dynamic-update-slice_fusion.2
  213.8 1.0 constant_dynamic-update-slice_fusion.1
  214.8 1.0 constant_dynamic-update-slice_fusion
  215.8 29.0 %all-gather.9.cloned.1.call-done = f32[3,1,512,1024]{3,2,0,1:T(8,128)} async-done(((f32[3,1,512,128]{3,2,0,1:T(8,128)}), f32[3,1,512,1024]{3,2,0,1:T(8,128)}) %all-gather.9.cloned.1.call-update) | async-done | bytes 6291472 | tf_op jit(solution)/shard_map/all_gather | solution.py:75
  244.8 7.9 %fusion.2 = f32[3,512,128]{2,1,0:T(8,128)S(1)} fusion(f32[3,1,512,1024]{3,2,0,1:T(8,128)} %all-gather.9.cloned.1.call-done, f32[3,1,1024,128]{3,2,0,1:T(8,128)} %all-gather.11.cloned.1.call-done), kind=kOutput, calls=%fused_computation.2 | convolution fusion | flops 2415919104 | bytes 8650752 | tf_op jit(solution)/shard_map/mgq,mqn->mgn/dot_general | solution.py:38
  252.7 90.1 %all-gather.7.cloned.1.call-done = f32[3,1,1024,128]{3,2,0,1:T(8,128)} async-done(((f32[3,1,512,128]{3,2,0,1:T(8,128)}), f32[3,1,1024,128]{3,2,0,1:T(8,128)}) %all-gather.7.cloned.1.call-update) | async-done | bytes 1572880 | tf_op jit(solution)/shard_map/all_gather | solution.py:71
  342.8 8.1 %fusion = f32[3,512,128]{2,1,0:T(8,128)S(1)} fusion(f32[3,1,512,1024]{3,2,0,1:T(8,128)} %all-gather.9.cloned.1.call-done, f32[3,1,1024,128]{3,2,0,1:T(8,128)} %all-gather.7.cloned.1.call-done), kind=kOutput, calls=%fused_computation | convolution fusion | flops 2415919104 | bytes 8650752 | tf_op jit(solution)/shard_map/mgq,mqn->mgn/dot_general | solution.py:38
  350.9 8.0 %fusion.17 = f32[1,3,512,128]{3,2,1,0:T(8,128)S(1)} fusion(f32[3,512,128]{2,1,0:T(8,128)S(1)} %fusion.2, f32[3,1,1024,128]{3,2,0,1:T(8,128)} %all-gather.7.cloned.1.call-done, f32[3,512,2048]{2,1,0:T(8,128)} %constant_dynamic-update-slice_fusion, s32[]{:T(128)S(6)} %select_n.34), kind=kOutput, calls=%fused_computation.14 | convolution fusion | flops 2416115712 | bytes 9437188 | tf_op jit(solution)/shard_map/mgq,mqn->mgn/dot_general | solution.py:38
  358.9 7.7 %fusion.27 = f32[1,3,512,128]{3,2,1,0:T(8,128)S(1)} fusion(f32[3,512,128]{2,1,0:T(8,128)S(1)} %fusion, f32[3,1,1024,128]{3,2,0,1:T(8,128)S(1)} %copy-done.3, f32[3,512,2048]{2,1,0:T(8,128)} %constant_dynamic-update-slice_fusion, s32[]{:T(128)S(6)} %select_n.34), kind=kOutput, calls=%fused_computation.16 | convolution fusion | flops 2416115712 | bytes 9437188 | tf_op jit(solution)/shard_map/mgq,mqn->mgn/dot_general | solution.py:38
  366.5 1.2 maximum_multiply_fusion
  (29 shorter events, 1.0 us)
Async XLA Ops:
  6.5 1.6 copy-start
  6.5 209.2 %all-gather.11.cloned.1.call-start = ((), (), s32[]{:S(2)}) async-start(), calls=%async_computation.3 | async-start | bytes 2359296 | tf_op jit(solution)/shard_map/all_gather | solution.py:72
  100.9 1.1 copy-start.1
  103.5 141.2 %all-gather.9.cloned.1.call-start = ((), (), s32[]{:S(2)}) async-start(), calls=%async_computation.2 | async-start | bytes 7077888 | tf_op jit(solution)/shard_map/all_gather | solution.py:75
  104.3 238.5 %all-gather.7.cloned.1.call-start = ((), (), s32[]{:S(2)}) async-start(), calls=%async_computation.1 | async-start | bytes 2359296 | tf_op jit(solution)/shard_map/all_gather | solution.py:71
  104.3 12.7 %collective-permute-start = (f32[3,512,128]{2,1,0:T(8,128)}, f32[3,512,128]{2,1,0:T(8,128)S(1)}, u32[]{:S(2)}, u32[]{:S(2)}) collective-permute-start(f32[3,512,128]{2,1,0:T(8,128)} %get-tuple-element.5), channel_id=1, source_target_pairs={{0,1},{1,2},{2,3},{3,4},{4,5},{5,6},{6,7},{7,0},{8,9},{9,10},{10,1... | collective-permute-start | bytes 2359304 | tf_op jit(solution)/shard_map/ppermute | solution.py:18
  117.0 11.3 %collective-permute-start.1 = (f32[3,512,128]{2,1,0:T(8,128)S(1)}, f32[3,512,128]{2,1,0:T(8,128)S(1)}, u32[]{:S(2)}, u32[]{:S(2)}) collective-permute-start(f32[3,512,128]{2,1,0:T(8,128)S(1)} %collective-permute-done), channel_id=1, source_target_pairs={{0,1},{1,2},{2,3},{3,4},{4,5},{5,6},{6,7},{7,0},{8,9},{9,10},{10,1... | collective-permute-start | bytes 2359304 | tf_op jit(solution)/shard_map/ppermute | solution.py:18
  128.3 0.9 copy-start.4
  129.2 11.4 %collective-permute-start.2 = (f32[3,512,128]{2,1,0:T(8,128)S(1)}, f32[3,512,128]{2,1,0:T(8,128)S(1)}, u32[]{:S(2)}, u32[]{:S(2)}) collective-permute-start(f32[3,512,128]{2,1,0:T(8,128)S(1)} %collective-permute-done.1), channel_id=1, source_target_pairs={{0,1},{1,2},{2,3},{3,4},{4,5},{5,6},{6,7},{7,0},{8,9},{9,10},{10,1... | collective-permute-start | bytes 2359304 | tf_op jit(solution)/shard_map/ppermute | solution.py:18
  140.6 1.0 copy-start.6
  141.6 11.4 %collective-permute-start.3 = (f32[3,512,128]{2,1,0:T(8,128)S(1)}, f32[3,512,128]{2,1,0:T(8,128)S(1)}, u32[]{:S(2)}, u32[]{:S(2)}) collective-permute-start(f32[3,512,128]{2,1,0:T(8,128)S(1)} %collective-permute-done.2), channel_id=1, source_target_pairs={{0,1},{1,2},{2,3},{3,4},{4,5},{5,6},{6,7},{7,0},{8,9},{9,10},{10,1... | collective-permute-start | bytes 2359304 | tf_op jit(solution)/shard_map/ppermute | solution.py:18
  153.0 1.0 copy-start.8
  154.0 11.4 %collective-permute-start.4 = (f32[3,512,128]{2,1,0:T(8,128)S(1)}, f32[3,512,128]{2,1,0:T(8,128)S(1)}, u32[]{:S(2)}, u32[]{:S(2)}) collective-permute-start(f32[3,512,128]{2,1,0:T(8,128)S(1)} %collective-permute-done.3), channel_id=1, source_target_pairs={{0,1},{1,2},{2,3},{3,4},{4,5},{5,6},{6,7},{7,0},{8,9},{9,10},{10,1... | collective-permute-start | bytes 2359304 | tf_op jit(solution)/shard_map/ppermute | solution.py:18
  165.4 0.9 copy-start.10
  166.3 11.4 %collective-permute-start.5 = (f32[3,512,128]{2,1,0:T(8,128)S(1)}, f32[3,512,128]{2,1,0:T(8,128)}, u32[]{:S(2)}, u32[]{:S(2)}) collective-permute-start(f32[3,512,128]{2,1,0:T(8,128)S(1)} %collective-permute-done.4), channel_id=1, source_target_pairs={{0,1},{1,2},{2,3},{3,4},{4,5},{5,6},{6,7},{7,0},{8,9},{9,10},{10,1... | collective-permute-start | bytes 2359304 | tf_op jit(solution)/shard_map/ppermute | solution.py:18
  177.7 11.8 %collective-permute-start.6 = (f32[3,512,128]{2,1,0:T(8,128)}, f32[3,512,128]{2,1,0:T(8,128)}, u32[]{:S(2)}, u32[]{:S(2)}) collective-permute-start(f32[3,512,128]{2,1,0:T(8,128)} %collective-permute-done.5), channel_id=1, source_target_pairs={{0,1},{1,2},{2,3},{3,4},{4,5},{5,6},{6,7},{7,0},{8,9},{9,10},{10,1... | collective-permute-start | bytes 2359304 | tf_op jit(solution)/shard_map/ppermute | solution.py:18
  180.3 29.5 %copy-start.11 = (f32[3,512,128]{2,1,0:T(8,128)S(1)}, f32[3,512,128]{2,1,0:T(8,128)}, u32[]{:S(2)}) copy-start(f32[3,512,128]{2,1,0:T(8,128)} %copy-done.10) | copy-start | bytes 2359300
  180.3 30.4 %copy-start.9 = (f32[3,512,128]{2,1,0:T(8,128)S(1)}, f32[3,512,128]{2,1,0:T(8,128)}, u32[]{:S(2)}) copy-start(f32[3,512,128]{2,1,0:T(8,128)} %copy-done.8) | copy-start | bytes 2359300
  180.3 31.5 %copy-start.7 = (f32[3,512,128]{2,1,0:T(8,128)S(1)}, f32[3,512,128]{2,1,0:T(8,128)}, u32[]{:S(2)}) copy-start(f32[3,512,128]{2,1,0:T(8,128)} %copy-done.6) | copy-start | bytes 2359300
  180.3 32.4 %copy-start.5 = (f32[3,512,128]{2,1,0:T(8,128)S(1)}, f32[3,512,128]{2,1,0:T(8,128)}, u32[]{:S(2)}) copy-start(f32[3,512,128]{2,1,0:T(8,128)} %copy-done.4) | copy-start | bytes 2359300
  180.3 34.4 %copy-start.2 = (f32[6,32,16,128]{3,2,1,0:T(8,128)S(1)}, f32[6,32,16,128]{3,2,1,0:T(8,128)}, u32[]{:S(2)}) copy-start(f32[6,32,16,128]{3,2,1,0:T(8,128)} %copy-done.1) | copy-start | bytes 4718596
  342.8 16.1 %copy-start.3 = (f32[3,1,1024,128]{3,2,0,1:T(8,128)S(1)}, f32[3,1,1024,128]{3,2,0,1:T(8,128)}, u32[]{:S(2)}) copy-start(f32[3,1,1024,128]{3,2,0,1:T(8,128)} %all-gather.11.cloned.1.call-done) | copy-start | bytes 4718596
Sparse Core Ops, SparseCore 0:
  103.6 92.2 all-gather.10
  198.0 46.6 all-gather.8
  246.9 95.8 all-gather.6
